TPU v7x, 256 devices: a whole 4x4x8 slice. The times are simulated.
256 devices in a mesh: dp: 2 (over z_hi), lat: 2 (over core), row: 64 (over z_lo, y, x).
Axes of the slice: x: 4, y: 4, z: 8 (z_hi: 2, z_lo: 4; z = z_hi * 4 + z_lo), core: 2. Of those that a mesh axis runs over, the one named last changes fastest.
Arguments:
- weight: float32 [5120, 16384], P('row', 'lat'), may hold values from -6 to 6
- grads: float32 [2, 5120, 16384], P('dp', 'row', 'lat'), may hold values from -11000 to 11000
- first: float32 [5120, 2, 8192], P('row', 'dp', 'lat'), may hold values from -4 to 4
- second: float32 [5120, 2, 8192], P('row', 'dp', 'lat'), may hold values from 0.04 to 1
Outputs:
- new_weight: float32 [5120, 16384], P('row', 'lat')
- new_first: float32 [5120, 2, 8192], P('row', 'dp', 'lat')
- new_second: float32 [5120, 2, 8192], P('row', 'dp', 'lat')
All inputs are finite; a program needn't handle non-finite values.
Results may differ from a plain program's by a relative error of at most 0.00002.
Values sent between devices are 32-bit elements; how exact they have to be, the bound alone decides.
A program may use at most 64 MiB of HBM per device.

v0:
```python
import jax
import jax.numpy as jnp
from jax import lax
from jax.sharding import PartitionSpec as P

D = 5120


def split_up(array, dim, size):
    before, after = (array.shape[:dim], array.shape[dim + 1 :])
    return jnp.moveaxis(array.reshape(*before, size, -1, *after), dim, 0)


def sum_at_owner(array, axis, dim):
    tiles = split_up(array, dim, lax.axis_size(axis))
    arrived = lax.all_to_all(tiles, axis, split_axis=0, concat_axis=0, tiled=True)
    return arrived.sum(axis=0)


def padded_to(lines, size):
    spare = -len(lines) % size
    return jnp.pad(lines, [(0, spare)] + [(0, 0)] * (lines.ndim - 1))


def copy_for_each(array, axis):
    size = lax.axis_size(axis)
    return lax.all_to_all(
        jnp.broadcast_to(array[None], (size, *array.shape)), axis, 0, 0, tiled=True
    )


def in_order(tiles, dim):
    tiles = jnp.moveaxis(tiles, 0, dim)
    shape = tiles.shape
    return tiles.reshape(*shape[:dim], shape[dim] * shape[dim + 1], *shape[dim + 2 :])


def gathered_copies(array, axis, dim):
    tiles = copy_for_each(array, axis)
    return in_order(tiles, dim)


def total_of(array, axes):
    padded = padded_to(array, lax.axis_size(axes))
    whole = gathered_copies(sum_at_owner(padded, axes, 0), axes, 0)
    return lax.slice_in_dim(whole, 0, len(array)).reshape(array.shape)


def packed_total(arrays, axis):
    ends = [0]
    for a in arrays:
        ends.append(ends[-1] + a.size)
    so_far = total_of(jnp.concatenate([a.ravel() for a in arrays]), axis)
    return tuple((so_far[b:e].reshape(a.shape) for a, b, e in zip(arrays, ends, ends[1:])))


def taken_together(array, axis):
    return copy_for_each(array, axis).sum(axis=0)


def per_device(weight, grads, first, second):
    summed = sum_at_owner(grads[0], "dp", 1)
    width = summed.shape[1]
    columns = lax.dynamic_slice_in_dim(weight, lax.axis_index("dp") * width, width, 1)
    entries = weight.shape[0] * lax.axis_size("row") * weight.shape[1] * lax.axis_size("lat")
    inner, length, squares = packed_total(
        (
            jnp.sum(columns * summed, axis=0),
            jnp.sum(columns * columns, axis=0),
            jnp.sum(summed * summed, axis=0),
        ),
        "row",
    )
    ratio = inner / length
    projected = summed - ratio[None, :] * columns
    total = taken_together(jnp.sum(squares - inner * ratio), ("dp", "lat"))
    spread = jnp.sqrt(total / entries + 1e-06)
    clip = jnp.minimum(jnp.float32(1.0), 0.5 / spread)
    clipped = clip * projected
    new_first = 0.9 * first[:, 0, :] + 0.1 * clipped
    new_second = 0.999 * second[:, 0, :] + 0.001 * clipped * clipped
    raw = columns - 0.2 * new_first / (jnp.sqrt(new_second) + 1e-08)
    sums = taken_together(jnp.sum(raw * raw, axis=0), "row")
    scaled = raw * lax.rsqrt(sums / D + 1e-06)[None, :]
    new_weight = gathered_copies(scaled, "dp", 1)
    return (new_weight, new_first[:, None, :], new_second[:, None, :])


def solution(mesh):
    return jax.shard_map(
        per_device,
        mesh=mesh,
        in_specs=(
            P("row", "lat"),
            P("dp", "row", "lat"),
            P("row", "dp", "lat"),
            P("row", "dp", "lat"),
        ),
        out_specs=(P("row", "lat"), P("row", "dp", "lat"), P("row", "dp", "lat")),
        check_vma=False,
    )
```

profile of v0, /device:TPU:2, one launch (start us, length us, event | category | flops | bytes accessed | tf_op | source)
XLA Modules:
  0.0 236.5 jit_solution(1708908477650107791)
XLA Ops:
  0.6 3.7 %reshape_squeeze.3 = f32[80,2,4096]{2,1,0:T(2,128)S(1)} reshape(f32[1,80,8192]{2,1,0:T(8,128)} %param.5) | data formatting | bytes 5242880 | tf_op jit(solution)/shard_map/reshape;squeeze | solution.py:11
  4.3 3.0 %copy.20 = f32[2,80,4096]{2,1,0:T(8,128)} copy(f32[2,80,4096]{2,0,1:T(2,128)S(1)} %bitcast.11) | data formatting | bytes 5242880 | tf_op jit(solution)/shard_map/transpose | solution.py:11
  7.3 8.5 %all-to-all-start = ((f32[2,80,4096]{2,1,0:T(8,128)}), f32[2,80,4096]{2,1,0:T(8,128)}, u32[]{:S(2)}, u32[]{:S(2)}) async-start(f32[2,80,4096]{2,1,0:T(8,128)} %copy.20), calls=%async_computation | async-start | bytes 5242880 | tf_op jit(solution)/shard_map/all_to_all | solution.py:16
  15.8 61.9 %all-to-all-done = f32[2,80,4096]{2,1,0:T(8,128)} async-done(((f32[2,80,4096]{2,1,0:T(8,128)}), f32[2,80,4096]{2,1,0:T(8,128)}, u32[]{:S(2)}, u32[]{:S(2)}) %all-to-all-start) | async-done | bytes 2621472 | tf_op jit(solution)/shard_map/all_to_all | solution.py:16
  77.6 2.0 reduce_sum.81
  79.7 1.7 multiply_reduce_fusion.3
  81.4 0.1 all_to_all.25
  81.5 18.5 %all_to_all.37 = f32[64,1,192]{2,1,0:T(1,128)S(1)} all-to-all(f32[64,1,192]{2,1,0:T(1,128)S(1)} %all_to_all.25), channel_id=1, replica_groups=mesh['dp'=2,'lat'=2,'row'=64] {'row'}, dimensions={0} | all-to-all | bytes 98304 | tf_op jit(solution)/shard_map/all_to_all | solution.py:16
  100.0 0.1 reduce_sum.85
  100.1 14.2 %all_to_all.38 = f32[64,1,192]{2,1,0:T(1,128)S(1)} all-to-all(f32[64,1,192]{2,1,0:T(1,128)S(1)} %broadcast_in_dim.12), channel_id=1, replica_groups=mesh['dp'=2,'lat'=2,'row'=64] {'row'}, dimensions={0} | all-to-all | bytes 98304 | tf_op jit(solution)/shard_map/all_to_all | solution.py:27
  114.3 0.2 reduce.3
  114.5 0.1 reshape.43
  114.6 0.6 fusion.1
  115.2 0.6 broadcast_in_dim.13
  115.8 10.0 %all_to_all.39 = f32[4,1,1]{2,1,0:T(1,128)S(1)} all-to-all(f32[4,1,1]{2,1,0:T(1,128)S(1)} %broadcast_in_dim.13), channel_id=1, replica_groups=mesh['dp'=2,'lat'=2,'row'=64] {'dp','lat'}, dimensions={0} | all-to-all | bytes 32 | tf_op jit(solution)/shard_map/all_to_all | solution.py:27
  125.8 0.6 reduce_sum.87
  127.1 6.3 %multiply_reduce_fusion = (f32[4096]{0:T(1024)S(1)}, f32[80,4096]{1,0:T(8,128)S(1)}, f32[80,4096]{1,0:T(8,128)}, f32[80,4096]{1,0:T(8,128)}) fusion(f32[80,8192]{1,0:T(8,128)} %param.4, s32[]{:T(128)S(6)} %select_n.3, f32[80,4096]{1,0:T(8,128)S(1)} %reduce_sum.81, f32[4096]{0:T(1024)S(1)} %get-tuple-element.11, f32[]{:T(128)S(6)} %min_shard_map.3, ...), kind=kLoop, calls=%fused_computation.5 | loop fusion | flops 5238784 | bytes 9207816 | tf_op jit(solution)/shard_map/reduce_sum | solution.py:83
  133.4 1.0 broadcast_in_dim.14
  134.4 33.1 %all_to_all.40 = f32[64,1,4096]{2,1,0:T(1,128)S(1)} all-to-all(f32[64,1,4096]{2,1,0:T(1,128)S(1)} %broadcast_in_dim.14), channel_id=1, replica_groups=mesh['dp'=2,'lat'=2,'row'=64] {'row'}, dimensions={0} | all-to-all | bytes 2097152 | tf_op jit(solution)/shard_map/all_to_all | solution.py:27
  167.5 0.9 reduce_sum.89
  168.4 0.1 broadcast_multiply_fusion
  168.5 1.8 broadcast_in_dim.15
  170.2 3.9 %all-to-all-start.5 = ((f32[2,80,4096]{2,1,0:T(8,128)}), f32[2,80,4096]{2,1,0:T(8,128)S(1)}, u32[]{:S(2)}, u32[]{:S(2)}) async-start(f32[2,80,4096]{2,1,0:T(8,128)} %broadcast_in_dim.15), calls=%async_computation.5 | async-start | bytes 5242880 | tf_op jit(solution)/shard_map/all_to_all | solution.py:27
  174.1 0.0 copy-start
  174.1 4.0 %broadcast_in_dim.16 = f32[80,1,4096]{2,1,0:T(1,128)} reshape(f32[80,4096]{1,0:T(8,128)} %get-tuple-element.8) | data formatting | bytes 2621440 | tf_op jit(solution)/shard_map/broadcast_in_dim | solution.py:86
  178.1 0.0 copy-done
  178.1 2.5 %broadcast_in_dim.17 = f32[80,1,4096]{2,1,0:T(1,128)} reshape(f32[80,4096]{1,0:T(8,128)S(1)} %copy-done) | data formatting | bytes 2621440 | tf_op jit(solution)/shard_map/broadcast_in_dim | solution.py:86
  180.6 54.2 %all-to-all-done.5 = f32[2,80,4096]{2,1,0:T(8,128)S(1)} async-done(((f32[2,80,4096]{2,1,0:T(8,128)}), f32[2,80,4096]{2,1,0:T(8,128)S(1)}, u32[]{:S(2)}, u32[]{:S(2)}) %all-to-all-start.5) | async-done | bytes 2621472 | tf_op jit(solution)/shard_map/all_to_all | solution.py:27
  234.8 1.7 copy.29
  (3 shorter events, 0.1 us)
Async XLA Ops:
  7.3 70.3 %all-to-all-start = ((f32[2,80,4096]{2,1,0:T(8,128)}), f32[2,80,4096]{2,1,0:T(8,128)}, u32[]{:S(2)}, u32[]{:S(2)}) async-start(f32[2,80,4096]{2,1,0:T(8,128)} %copy.20), calls=%async_computation | async-start | bytes 5242880 | tf_op jit(solution)/shard_map/all_to_all | solution.py:16
  170.2 64.6 %all-to-all-start.5 = ((f32[2,80,4096]{2,1,0:T(8,128)}), f32[2,80,4096]{2,1,0:T(8,128)S(1)}, u32[]{:S(2)}, u32[]{:S(2)}) async-start(f32[2,80,4096]{2,1,0:T(8,128)} %broadcast_in_dim.15), calls=%async_computation.5 | async-start | bytes 5242880 | tf_op jit(solution)/shard_map/all_to_all | solution.py:27
  174.1 4.0 %copy-start = (f32[80,4096]{1,0:T(8,128)S(1)}, f32[80,4096]{1,0:T(8,128)}, u32[]{:S(2)}) copy-start(f32[80,4096]{1,0:T(8,128)} %get-tuple-element.9) | copy-start | bytes 3932164
where the time goes:
time: 237 us; the launch traced here: 236 us
  waiting for transfers between devices  116 us (49%)
  blocking collectives  75.8 us (32%)
  local copies, waits for them, and re-layouts  18.5 us (8%)
  other arithmetic  12.4 us (5%)
  starting transfers between devices  12.3 us (5%)
    all_to_all x1, waiting for transfers between devices, sum_at_owner(): lax.all_to_all(tiles, axis, split_axis=0, concat_axis=0, tiled=True)  61.9 us
    all_to_all x3, blocking collectives, copy_for_each(): lax.all_to_all(jnp.broadcast_to(array[None], (size, *array.shape)), axis,...  57.3 us
    all_to_all x1, waiting for transfers between devices, copy_for_each(): lax.all_to_all(jnp.broadcast_to(array[None], (size, *array.shape)), axis,...  54.2 us
    all_to_all x1, blocking collectives, sum_at_owner(): lax.all_to_all(tiles, axis, split_axis=0, concat_axis=0, tiled=True)  18.5 us
    all_to_all x1, starting transfers between devices, sum_at_owner(): lax.all_to_all(tiles, axis, split_axis=0, concat_axis=0, tiled=True)  8.46 us
    broadcast_in_dim x2, local copies, waits for them, and re-layouts, per_device(): return (new_weight, new_first[:, None, :], new_second[:, None, :])  6.49 us
    reduce_sum x1, other arithmetic, per_device(): sums = taken_together(jnp.sum(raw * raw, axis=0), 'row')  6.27 us
  transfers between devices with their start and end apart: 2, of which 2 were waited for; matrix products, arithmetic and copies ran while one was open for 3% of the time, Pallas kernels for 0%

commit v1 on v0

v1 whole, which is shorter than its diff:
```python
import functools

import jax
import jax.numpy as jnp
from jax import lax
from jax.experimental import pallas as pl
from jax.experimental.pallas import tpu as pltpu
from jax.sharding import PartitionSpec as P

MESH = pl.DeviceIdType.MESH
F32 = jnp.float32
PLANE = 16
Z_LO = 4
BLK = 256
ROWS = 8


def each(low, high, body):
    def step(k, carry):
        body(k)
        return carry

    lax.fori_loop(low, high, step, 0)


def comm(
    depth, entries, w_h, g_h, f_h, s_h, nw, nf, ns,
    w_own, w_oth, g_own, g_oth, fv, sv, got1, proj, raw, got2, norms,
    st, rs1, z1, zs, zo, ratio, sa, sb, cst, rs2, z2, scale,
    load, b1s, b1r, b2s, b2r, small_s, small_r,
):
    rows, half = w_own.shape
    chunks, blocks = rows // ROWS, half // BLK
    dp, lat, row = lax.axis_index("dp"), lax.axis_index("lat"), lax.axis_index("row")
    zlo, q = row // PLANE, lax.rem(row, PLANE)
    z8 = dp * Z_LO + zlo
    u = lat * 8 + z8
    own = pl.multiple_of(dp * half, half)
    oth = pl.multiple_of((1 - dp) * half, half)
    partner = (1 - dp, lat, row)

    def in_plane(k):
        return (dp, lat, zlo * PLANE + lax.rem(q + k, PLANE))

    def along_z(k):
        z = lax.rem(z8 + k, 8)
        return (z // Z_LO, lat, lax.rem(z, Z_LO) * PLANE + q)

    def column(k):
        v = lax.rem(u + k, 16)
        z = lax.rem(v, 8)
        return (z // Z_LO, v // 8, lax.rem(z, Z_LO) * PLANE + q)

    def same_half(j):
        return (dp, lat, lax.rem(zlo + j, Z_LO) * PLANE + q)

    def other_half(j):
        return (1 - dp, lat, lax.rem(zlo + j, Z_LO) * PLANE + q)

    def remote(src, dst, s, r, device):
        return pltpu.make_async_remote_copy(
            src_ref=src, dst_ref=dst, send_sem=s, recv_sem=r, device_id=device, device_id_type=MESH
        )

    def fetch(src, dst, i):
        return pltpu.make_async_copy(src, dst, load.at[i])

    fetches = [
        fetch(w_h.at[:, pl.ds(own, half)], w_own, 0),
        fetch(g_h.at[0, :, pl.ds(own, half)], g_own, 1),
        fetch(w_h.at[:, pl.ds(oth, half)], w_oth, 2),
        fetch(g_h.at[0, :, pl.ds(oth, half)], g_oth, 3),
        fetch(f_h.at[:, 0, :], fv, 4),
        fetch(s_h.at[:, 0, :], sv, 5),
    ]
    for f in fetches:
        f.start()

    barrier = pltpu.get_barrier_semaphore()

    def greet(k):
        pl.semaphore_signal(barrier, inc=1, device_id=in_plane(k), device_id_type=MESH)
        pl.semaphore_signal(barrier, inc=1, device_id=column(k), device_id_type=MESH)

    each(1, 16, greet)
    pl.semaphore_wait(barrier, 30)

    def bulk1(i):
        at = pl.ds(pl.multiple_of(i * ROWS, ROWS), ROWS)
        return remote(g_oth.at[at], got1.at[at], b1s.at[i], b1r.at[i], partner)

    def bulk2(i):
        at = pl.ds(pl.multiple_of(i * ROWS, ROWS), ROWS)
        return remote(raw.at[at], got2.at[at], b2s.at[i], b2r.at[i], partner)

    fetches[3].wait()
    each(0, chunks, lambda i: bulk1(i).start())

    fetches[0].wait()
    fetches[1].wait()

    def own_sums(b):
        at = pl.ds(pl.multiple_of(b * BLK, BLK), BLK)
        w = w_own[:, at]
        st[b, 1] = jnp.sum(w * g_own[:, at], axis=0, keepdims=True)
        st[b, 2] = jnp.sum(w * w, axis=0, keepdims=True)

    each(0, blocks, own_sums)
    fetches[2].wait()

    def other_sums(b):
        at = pl.ds(pl.multiple_of(b * BLK, BLK), BLK)
        st[b, 0] = jnp.sum(w_oth[:, at] * g_oth[:, at], axis=0, keepdims=True)

    each(0, blocks, other_sums)

    def scatter(src, dst, stage):
        def copy(k):
            return remote(
                src.at[lax.rem(q + k, PLANE)], dst.at[q],
                small_s.at[stage, k], small_r.at[stage, k], in_plane(k),
            )

        return copy

    def gather(ref, stage):
        def copy(k):
            return remote(ref.at[q], ref.at[q], small_s.at[stage, k], small_r.at[stage, k], in_plane(k))

        return copy

    def run(copy, low, high):
        each(low, high, lambda k: copy(k).start())
        each(low, high, lambda k: copy(k).wait_recv())

    rs1[q] = st[q]
    scatter1 = scatter(st, rs1, 0)
    run(scatter1, 1, PLANE)
    z1[...] = jnp.sum(rs1[...], axis=0)

    def same_copy(j):
        return remote(z1.at[pl.ds(1, 2)], zs.at[zlo], small_s.at[1, j], small_r.at[1, j], same_half(j))

    def other_copy(j):
        return remote(z1.at[pl.ds(0, 1)], zo.at[zlo], small_s.at[1, 8 + j], small_r.at[1, 8 + j], other_half(j))

    zs[zlo] = z1[1:3]
    each(1, Z_LO, lambda j: same_copy(j).start())
    each(0, Z_LO, lambda j: other_copy(j).start())
    each(1, Z_LO, lambda j: same_copy(j).wait_recv())
    each(0, Z_LO, lambda j: other_copy(j).wait_recv())
    same = jnp.sum(zs[...], axis=0)
    inner = same[0] + jnp.sum(zo[...], axis=0)[0]
    ratio[q] = inner / same[1]
    gather1 = gather(ratio, 2)
    run(gather1, 1, PLANE)

    def project(i, total):
        bulk1(i).wait_recv()
        at = pl.ds(pl.multiple_of(i * ROWS, ROWS), ROWS)
        for b in range(blocks):
            cols = pl.ds(b * BLK, BLK)
            p = (g_own[at, cols] + got1[at, cols]) - ratio[b] * w_own[at, cols]
            proj[at, cols] = p
            total = total + p * p
        return total

    total = lax.fori_loop(0, chunks, project, jnp.zeros((ROWS, BLK), F32))
    total = jnp.sum(total, axis=0, keepdims=True)
    sa[q] = total[:, :128] + total[:, 128:]
    gather_a = gather(sa, 3)
    run(gather_a, 1, PLANE)
    sb[u] = jnp.sum(sa[...], axis=0)

    def gather_b(k):
        return remote(sb.at[u], sb.at[u], small_s.at[4, k], small_r.at[4, k], column(k))

    run(gather_b, 1, 16)
    total = jnp.sum(jnp.sum(sb[...], axis=0), axis=1, keepdims=True)
    clip = jnp.minimum(F32(1.0), 0.5 / jnp.sqrt(total / entries + 1e-06))

    fetches[4].wait()
    fetches[5].wait()
    norms[...] = jnp.zeros_like(norms)

    def update(i):
        at = pl.ds(pl.multiple_of(i * ROWS, ROWS), ROWS)
        for b in range(blocks):
            cols = pl.ds(b * BLK, BLK)
            clipped = clip * proj[at, cols]
            first = 0.9 * fv[at, cols] + 0.1 * clipped
            second = 0.999 * sv[at, cols] + 0.001 * clipped * clipped
            nf[at, cols] = first
            ns[at, cols] = second
            r = w_own[at, cols] - 0.2 * first / (jnp.sqrt(second) + 1e-08)
            raw[at, cols] = r
            norms[:, cols] += r * r
        bulk2(i).start()

    each(0, chunks, update)
    for b in range(blocks):
        cst[b] = jnp.sum(norms[:, pl.ds(b * BLK, BLK)], axis=0, keepdims=True)
    rs2[q] = cst[q]
    scatter2 = scatter(cst, rs2, 5)
    run(scatter2, 1, PLANE)
    z2[z8] = jnp.sum(rs2[...], axis=0)

    def gather_z(k):
        return remote(z2.at[z8], z2.at[z8], small_s.at[6, k], small_r.at[6, k], along_z(k))

    run(gather_z, 1, 8)
    for h in range(2):
        whole = jnp.sum(z2[h * Z_LO : (h + 1) * Z_LO], axis=0)
        scale[q, h] = lax.rsqrt(whole / depth + 1e-06)
    gather2 = gather(scale, 7)
    run(gather2, 1, PLANE)

    def finish(src, part, base):
        def step(i):
            at = pl.ds(pl.multiple_of(i * ROWS, ROWS), ROWS)
            for b in range(blocks):
                cols = pl.ds(pl.multiple_of(base + b * BLK, BLK), BLK)
                nw[at, cols] = src[at, pl.ds(b * BLK, BLK)] * scale[b, part]

        return step

    each(0, chunks, finish(raw, dp, own))
    last = finish(got2, 1 - dp, oth)

    def receive(i):
        bulk2(i).wait_recv()
        last(i)

    each(0, chunks, receive)

    each(0, chunks, lambda i: bulk1(i).wait_send())
    each(0, chunks, lambda i: bulk2(i).wait_send())
    for copy in (scatter1, gather1, gather_a, gather_b, scatter2, gather2):
        each(1, PLANE, lambda k: copy(k).wait_send())
    each(1, 8, lambda k: gather_z(k).wait_send())
    each(1, Z_LO, lambda j: same_copy(j).wait_send())
    each(0, Z_LO, lambda j: other_copy(j).wait_send())


def store(nw, nf, ns, nw_h, nf_h, ns_h, sem):
    copies = [
        pltpu.make_async_copy(nw, nw_h, sem.at[0]),
        pltpu.make_async_copy(nf, nf_h.at[:, 0, :], sem.at[1]),
        pltpu.make_async_copy(ns, ns_h.at[:, 0, :], sem.at[2]),
    ]
    for c in copies:
        c.start()
    for c in copies:
        c.wait()


def solution(mesh):
    def step(weight, grads, first, second):
        rows, width = weight.shape
        half = width // mesh.shape["dp"]
        depth = rows * mesh.shape["row"]
        entries = depth * width * mesh.shape["lat"]
        vmem = pl.BlockSpec(memory_space=pltpu.VMEM)
        hbm = pl.BlockSpec(memory_space=pltpu.HBM)
        tile = pltpu.VMEM((rows, half), F32)
        chunks = rows // ROWS
        dma = pltpu.SemaphoreType.DMA
        new_weight, new_first, new_second = pl.pallas_call(
            functools.partial(comm, depth, entries),
            out_shape=(
                jax.ShapeDtypeStruct((rows, width), F32),
                jax.ShapeDtypeStruct((rows, half), F32),
                jax.ShapeDtypeStruct((rows, half), F32),
            ),
            in_specs=[hbm] * 4,
            out_specs=[vmem] * 3,
            scratch_shapes=[
                *[tile] * 10,
                pltpu.VMEM((ROWS, half), F32),
                pltpu.VMEM((PLANE, 3, 1, BLK), F32),
                pltpu.VMEM((PLANE, 3, 1, BLK), F32),
                pltpu.VMEM((3, 1, BLK), F32),
                pltpu.VMEM((Z_LO, 2, 1, BLK), F32),
                pltpu.VMEM((Z_LO, 1, 1, BLK), F32),
                pltpu.VMEM((PLANE, 1, BLK), F32),
                pltpu.VMEM((PLANE, 1, 128), F32),
                pltpu.VMEM((16, 1, 128), F32),
                pltpu.VMEM((PLANE, 1, BLK), F32),
                pltpu.VMEM((PLANE, 1, BLK), F32),
                pltpu.VMEM((8, 1, BLK), F32),
                pltpu.VMEM((PLANE, 2, 1, BLK), F32),
                dma((6,)),
                dma((chunks,)),
                dma((chunks,)),
                dma((chunks,)),
                dma((chunks,)),
                dma((8, 16)),
                dma((8, 16)),
            ],
            compiler_params=pltpu.CompilerParams(
                collective_id=0, has_side_effects=True, vmem_limit_bytes=24 << 20
            ),
        )(*[pltpu.with_memory_space_constraint(a, pltpu.HBM) for a in (weight, grads, first, second)])
        return pl.pallas_call(
            store,
            out_shape=(
                jax.ShapeDtypeStruct(weight.shape, F32),
                jax.ShapeDtypeStruct(first.shape, F32),
                jax.ShapeDtypeStruct(second.shape, F32),
            ),
            in_specs=[vmem] * 3,
            out_specs=[hbm] * 3,
            scratch_shapes=[dma((3,))],
            compiler_params=pltpu.CompilerParams(vmem_limit_bytes=16 << 20),
        )(new_weight, new_first, new_second)

    return jax.shard_map(
        step,
        mesh=mesh,
        in_specs=(P("row", "lat"), P("dp", "row", "lat"), P("row", "dp", "lat"), P("row", "dp", "lat")),
        out_specs=(P("row", "lat"), P("row", "dp", "lat"), P("row", "dp", "lat")),
        check_vma=False,
    )
```

time: 237 us -> 156 us (0.66)
  Pallas kernels: 0 us -> 155 us
  waiting for transfers between devices: 116 us -> 0 us
  blocking collectives: 75.8 us -> 0 us
  local copies, waits for them, and re-layouts: 18.5 us -> 0 us
  other arithmetic: 12.4 us -> 0 us
  starting transfers between devices: 12.3 us -> 0 us
    pallas_call x0 -> x2, Pallas kernels: none -> 155 us  [the longest x1 153 us: step(): pl.pallas_call(functools.partial(comm, depth, entries), out_shape=(jax.Sh...]
    all_to_all x2 -> x0, waiting for transfers between devices: 116 us -> none  [the longest x1 61.9 us: sum_at_owner(): lax.all_to_all(tiles, axis, split_axis=0, concat_axis=0, tiled=True)]
    all_to_all x4 -> x0, blocking collectives: 75.8 us -> none  [the longest x3 57.3 us: copy_for_each(): lax.all_to_all(jnp.broadcast_to(array[None], (size, *array.shape)), axis,...]
    all_to_all x2 -> x0, starting transfers between devices: 12.3 us -> none  [the longest x1 8.46 us: sum_at_owner(): lax.all_to_all(tiles, axis, split_axis=0, concat_axis=0, tiled=True)]
    reduce_sum x7 -> x0, other arithmetic: 12.2 us -> none  [the longest x1 6.27 us: per_device(): sums = taken_together(jnp.sum(raw * raw, axis=0), 'row')]
    broadcast_in_dim x6 -> x0, local copies, waits for them, and re-layouts: 9.95 us -> none  [the longest x2 6.49 us: per_device(): return (new_weight, new_first[:, None, :], new_second[:, None, :])]
    another operation x1 -> x0, local copies, waits for them, and re-layouts: 3.66 us -> none  [split_up(): return jnp.moveaxis(array.reshape(*before, size, -1, *after), dim, 0)]
    transpose x1 -> x0, local copies, waits for them, and re-layouts: 3.02 us -> none  [split_up(): return jnp.moveaxis(array.reshape(*before, size, -1, *after), dim, 0)]
  transfers between devices with their start and end apart: 2 -> 0, of which waited for: 2 -> 0; matrix products, arithmetic and copies ran while one was open for 3% -> 0% of each run, Pallas kernels for 0% -> 0%
where the time goes in v1:
time: 156 us
  Pallas kernels  155 us (99%)
    pallas_call x1, Pallas kernels, step(): pl.pallas_call(functools.partial(comm, depth, entries), out_shape=(jax.Sh...  153 us

profile of v1, /device:TPU:2, one launch (start us, length us, event | category | flops | bytes accessed | tf_op | source)
XLA Modules:
  0.0 155.6 jit_solution(17495009350644368641)
XLA Ops:
  0.6 152.6 %shard_map.67 = (f32[80,8192]{1,0:T(8,128)S(1)}, f32[80,4096]{1,0:T(8,128)S(1)}, f32[80,4096]{1,0:T(8,128)S(1)}) custom-call(f32[80,8192]{1,0:T(8,128)} %w_h.1, f32[1,80,8192]{2,1,0:T(8,128)} %g_h.1, f32[80,1,4096]{2,1,0:T(1,128)} %f_h.1, f32[80,1,4096]{2,1,0:T(1,128)} %s_h.1), custom_call_target="tpu_custom_call" | custom-call | tf_op jit(solution)/shard_map/pallas_call | solution.py:268
  153.3 2.4 %shard_map.68 = (f32[80,8192]{1,0:T(8,128)}, f32[80,1,4096]{2,1,0:T(1,128)}, f32[80,1,4096]{2,1,0:T(1,128)}) custom-call(f32[80,8192]{1,0:T(8,128)S(1)} %get-tuple-element.6.nw, f32[80,4096]{1,0:T(8,128)S(1)} %get-tuple-element.7.nf, f32[80,4096]{1,0:T(8,128)S(1)} %get-tuple-element.8.ns), custom_call_target="tpu_custom_call" | custom-call | tf_op jit(solution)/shard_map/pallas_call | solution.py:304

commit v2 on v1

v2 whole, which is shorter than its diff:
```python
import functools

import jax
import jax.numpy as jnp
from jax import lax
from jax.experimental import pallas as pl
from jax.experimental.pallas import tpu as pltpu
from jax.sharding import PartitionSpec as P

MESH = pl.DeviceIdType.MESH
F32 = jnp.float32
PLANE = 16
Z_LO = 4
BLK = 256
ROWS = 8
HOPS = 4

def each(low, high, body):
    def step(k, carry):
        body(k)
        return carry

    lax.fori_loop(low, high, step, 0)


def comm(
    depth, entries, w_h, g_h, f_h, s_h, nw, nf, ns,
    w_own, w_oth, g_own, g_oth, fv, sv, grad, raw, norms, ring1, ring2,
    st, rs, col, ratio, plane, cst, pn, zn, scale,
    load, b1s, b1r, b2s, b2r, small_s, small_r,
):
    rows, half = w_own.shape
    chunks, blocks = rows // ROWS, half // BLK
    dp, lat, row = lax.axis_index("dp"), lax.axis_index("lat"), lax.axis_index("row")
    zlo, q = row // PLANE, lax.rem(row, PLANE)
    z8 = dp * Z_LO + zlo
    u = lat * 8 + z8
    own = pl.multiple_of(dp * half, half)
    oth = pl.multiple_of((1 - dp) * half, half)

    def in_plane(k):
        return (dp, lat, zlo * PLANE + lax.rem(q + k, PLANE))

    def column(k):
        v = lax.rem(u + k, 16)
        z = lax.rem(v, 8)
        return (z // Z_LO, v // 8, lax.rem(z, Z_LO) * PLANE + q)

    def along_z(k):
        z = lax.rem(z8 + k, 8)
        return (z // Z_LO, lat, lax.rem(z, Z_LO) * PLANE + q)

    onward = along_z(1 + 6 * lat)

    def remote(src, dst, s, r, device):
        return pltpu.make_async_remote_copy(
            src_ref=src, dst_ref=dst, send_sem=s, recv_sem=r, device_id=device, device_id_type=MESH
        )

    def fetch(src, dst, i):
        return pltpu.make_async_copy(src, dst, load.at[i])

    fetches = [
        fetch(w_h.at[:, pl.ds(own, half)], w_own, 0),
        fetch(g_h.at[0, :, pl.ds(own, half)], g_own, 1),
        fetch(w_h.at[:, pl.ds(oth, half)], w_oth, 2),
        fetch(g_h.at[0, :, pl.ds(oth, half)], g_oth, 3),
        fetch(f_h.at[:, 0, :], fv, 4),
        fetch(s_h.at[:, 0, :], sv, 5),
    ]
    for f in fetches:
        f.start()

    barrier = pltpu.get_barrier_semaphore()

    def greet(k):
        pl.semaphore_signal(barrier, inc=1, device_id=in_plane(k), device_id_type=MESH)
        pl.semaphore_signal(barrier, inc=1, device_id=column(k), device_id_type=MESH)

    each(1, 16, greet)

    def rows_of(i):
        return pl.ds(pl.multiple_of(i * ROWS, ROWS), ROWS)

    def bulk1(hop, i):
        at = rows_of(i)
        src = ring1.at[hop - 1, at] if hop else g_h.at[0, at, pl.ds(oth, half)]
        return remote(src, ring1.at[hop, at], b1s.at[hop, i], b1r.at[hop, i], onward)

    def bulk2(hop, i):
        at = rows_of(i)
        src = ring2.at[hop - 1, at] if hop else raw.at[at]
        return remote(src, ring2.at[hop, at], b2s.at[hop, i], b2r.at[hop, i], onward)

    def forward(bulk, hop, low, high):
        def one(i):
            bulk(hop - 1, i).wait_recv()
            bulk(hop, i).start()

        each(low, high, one)

    fetches[0].wait()
    fetches[1].wait()

    def own_sums(b):
        at = pl.ds(pl.multiple_of(b * BLK, BLK), BLK)
        w = w_own[:, at]
        st[b, dp] = jnp.sum(w * g_own[:, at], axis=0, keepdims=True)
        st[b, 2] = jnp.sum(w * w, axis=0, keepdims=True)

    each(0, blocks, own_sums)
    fetches[2].wait()
    fetches[3].wait()

    def other_sums(b):
        at = pl.ds(pl.multiple_of(b * BLK, BLK), BLK)
        st[b, 1 - dp] = jnp.sum(w_oth[:, at] * g_oth[:, at], axis=0, keepdims=True)

    each(0, blocks, other_sums)
    pl.semaphore_wait(barrier, 30)

    each(0, chunks, lambda i: bulk1(0, i).start())

    def scatter(src, dst, stage):
        def copy(k):
            to = lax.rem(q + k, PLANE)
            return remote(src.at[to], dst.at[q], small_s.at[stage, k], small_r.at[stage, k], in_plane(k))

        return copy

    def gather(ref, stage):
        def copy(k):
            return remote(ref.at[q], ref.at[q], small_s.at[stage, k], small_r.at[stage, k], in_plane(k))

        return copy

    def run(copy, low, high):
        each(low, high, lambda k: copy(k).start())
        each(low, high, lambda k: copy(k).wait_recv())

    rs[q] = st[q]
    scatter1 = scatter(st, rs, 0)
    run(scatter1, 1, PLANE)
    col[u, 0:3] = jnp.sum(rs[...], axis=0)
    for hop in range(1, HOPS):
        forward(bulk1, hop, 0, chunks)

    def add_up(i, total):
        bulk1(HOPS - 1, i).wait_recv()
        at = rows_of(i)
        for b in range(blocks):
            cols = pl.ds(b * BLK, BLK)
            p = g_own[at, cols] + ring1[HOPS - 1, at, cols]
            grad[at, cols] = p
            total = total + p * p
        return total

    total = lax.fori_loop(0, chunks, add_up, jnp.zeros((ROWS, BLK), F32))
    col[u, 3] = jnp.sum(total, axis=0, keepdims=True)

    def gather_z(k):
        return remote(col.at[u], col.at[u], small_s.at[1, k], small_r.at[1, k], column(k))

    run(gather_z, 1, 16)
    total = jnp.zeros((1, BLK), F32)
    for core in range(2):
        parts = [jnp.sum(col[pl.ds(core * 8 + h * Z_LO, Z_LO)], axis=0) for h in range(2)]
        for h in range(2):
            inner = parts[0][h] + parts[1][h]
            ratio[core, h] = inner / parts[h][2]
            total += parts[h][3] - inner * ratio[core, h]
    plane[q, 0] = ratio[lat, dp]
    plane[q, 1] = total
    gather1 = gather(plane, 2)
    run(gather1, 1, PLANE)
    total = jnp.sum(jnp.sum(plane[:, 1], axis=0), axis=1, keepdims=True)
    total = jnp.maximum(total, 0.0)
    clip = jnp.minimum(F32(1.0), 0.5 / jnp.sqrt(total / entries + 1e-06))

    fetches[4].wait()
    fetches[5].wait()
    norms[...] = jnp.zeros_like(norms)

    def update(i):
        at = rows_of(i)
        for b in range(blocks):
            cols = pl.ds(b * BLK, BLK)
            w = w_own[at, cols]
            clipped = clip * (grad[at, cols] - plane[b, 0] * w)
            first = 0.9 * fv[at, cols] + 0.1 * clipped
            second = 0.999 * sv[at, cols] + 0.001 * clipped * clipped
            nf[at, cols] = first
            ns[at, cols] = second
            r = w - 0.2 * first / (jnp.sqrt(second) + 1e-08)
            raw[at, cols] = r
            norms[:, cols] += r * r
        bulk2(0, i).start()

    each(0, chunks, update)
    for b in range(blocks):
        cst[b] = jnp.sum(norms[:, pl.ds(b * BLK, BLK)], axis=0, keepdims=True)

    pn[q] = cst[q]
    scatter2 = scatter(cst, pn, 3)
    run(scatter2, 1, PLANE)
    zn[z8] = jnp.sum(pn[...], axis=0)

    def gather_n(k):
        return remote(zn.at[z8], zn.at[z8], small_s.at[4, k], small_r.at[4, k], along_z(k))

    each(1, 8, lambda k: gather_n(k).start())
    forward(bulk2, 1, 0, chunks)
    forward(bulk2, 2, 0, chunks // 2)
    each(1, 8, lambda k: gather_n(k).wait_recv())
    for h in range(2):
        scale[q, h] = lax.rsqrt(jnp.sum(zn[h * Z_LO : (h + 1) * Z_LO], axis=0) / depth + 1e-06)
    gather2 = gather(scale, 5)
    each(1, PLANE, lambda k: gather2(k).start())
    forward(bulk2, 2, chunks // 2, chunks)
    each(1, PLANE, lambda k: gather2(k).wait_recv())

    def finish(src, part, base):
        def step(i):
            at = rows_of(i)
            for b in range(blocks):
                cols = pl.ds(pl.multiple_of(base + b * BLK, BLK), BLK)
                nw[at, cols] = src[at, pl.ds(b * BLK, BLK)] * scale[b, part]

        return step

    each(0, chunks, finish(raw, dp, own))
    forward(bulk2, 3, 0, chunks)
    last = finish(ring2.at[HOPS - 1], 1 - dp, oth)

    def receive(i):
        bulk2(HOPS - 1, i).wait_recv()
        last(i)

    each(0, chunks, receive)

    for hop in range(HOPS):
        each(0, chunks, lambda i: bulk1(hop, i).wait_send())
        each(0, chunks, lambda i: bulk2(hop, i).wait_send())
    for copy in (scatter1, gather_z, gather1, scatter2, gather2):
        each(1, PLANE, lambda k: copy(k).wait_send())
    each(1, 8, lambda k: gather_n(k).wait_send())


def store(nw, nf, ns, nw_h, nf_h, ns_h, sem):
    copies = [
        pltpu.make_async_copy(nw, nw_h, sem.at[0]),
        pltpu.make_async_copy(nf, nf_h.at[:, 0, :], sem.at[1]),
        pltpu.make_async_copy(ns, ns_h.at[:, 0, :], sem.at[2]),
    ]
    for c in copies:
        c.start()
    for c in copies:
        c.wait()


def solution(mesh):
    def step(weight, grads, first, second):
        rows, width = weight.shape
        half = width // mesh.shape["dp"]
        depth = rows * mesh.shape["row"]
        entries = depth * width * mesh.shape["lat"]
        vmem = pl.BlockSpec(memory_space=pltpu.VMEM)
        hbm = pl.BlockSpec(memory_space=pltpu.HBM)
        tile = pltpu.VMEM((rows, half), F32)
        chunks = rows // ROWS
        dma = pltpu.SemaphoreType.DMA
        new_weight, new_first, new_second = pl.pallas_call(
            functools.partial(comm, depth, entries),
            out_shape=(
                jax.ShapeDtypeStruct((rows, width), F32),
                jax.ShapeDtypeStruct((rows, half), F32),
                jax.ShapeDtypeStruct((rows, half), F32),
            ),
            in_specs=[hbm] * 4,
            out_specs=[vmem] * 3,
            scratch_shapes=[
                *[tile] * 8,
                pltpu.VMEM((ROWS, half), F32),
                pltpu.VMEM((HOPS, rows, half), F32),
                pltpu.VMEM((HOPS, rows, half), F32),
                pltpu.VMEM((PLANE, 3, 1, BLK), F32),
                pltpu.VMEM((PLANE, 3, 1, BLK), F32),
                pltpu.VMEM((16, 4, 1, BLK), F32),
                pltpu.VMEM((2, 2, 1, BLK), F32),
                pltpu.VMEM((PLANE, 2, 1, BLK), F32),
                pltpu.VMEM((PLANE, 1, BLK), F32),
                pltpu.VMEM((PLANE, 1, BLK), F32),
                pltpu.VMEM((8, 1, BLK), F32),
                pltpu.VMEM((PLANE, 2, 1, BLK), F32),
                dma((6,)),
                dma((HOPS, chunks)),
                dma((HOPS, chunks)),
                dma((HOPS, chunks)),
                dma((HOPS, chunks)),
                dma((6, 16)),
                dma((6, 16)),
            ],
            compiler_params=pltpu.CompilerParams(
                collective_id=0, has_side_effects=True, vmem_limit_bytes=32 << 20
            ),
        )(*[pltpu.with_memory_space_constraint(a, pltpu.HBM) for a in (weight, grads, first, second)])
        return pl.pallas_call(
            store,
            out_shape=(
                jax.ShapeDtypeStruct(weight.shape, F32),
                jax.ShapeDtypeStruct(first.shape, F32),
                jax.ShapeDtypeStruct(second.shape, F32),
            ),
            in_specs=[vmem] * 3,
            out_specs=[hbm] * 3,
            scratch_shapes=[dma((3,))],
            compiler_params=pltpu.CompilerParams(vmem_limit_bytes=16 << 20),
        )(new_weight, new_first, new_second)

    return jax.shard_map(
        step,
        mesh=mesh,
        in_specs=(P("row", "lat"), P("dp", "row", "lat"), P("row", "dp", "lat"), P("row", "dp", "lat")),
        out_specs=(P("row", "lat"), P("row", "dp", "lat"), P("row", "dp", "lat")),
        check_vma=False,
    )
```

time: 156 us -> 145 us (0.929)
  Pallas kernels: 155 us -> 144 us
    pallas_call x1, Pallas kernels: 153 us -> 142 us  [step(): pl.pallas_call(functools.partial(comm, depth, entries), out_shape=(jax.Sh...]
where the time goes in v2:
time: 145 us
  Pallas kernels  144 us (99%)
    pallas_call x1, Pallas kernels, step(): pl.pallas_call(functools.partial(comm, depth, entries), out_shape=(jax.Sh...  142 us

profile of v2, /device:TPU:2, one launch (start us, length us, event | category | flops | bytes accessed | tf_op | source)
XLA Modules:
  0.0 145.1 jit_solution(1697049461381718286)
XLA Ops:
  0.6 142.1 %shard_map.67 = (f32[80,8192]{1,0:T(8,128)S(1)}, f32[80,4096]{1,0:T(8,128)S(1)}, f32[80,4096]{1,0:T(8,128)S(1)}) custom-call(f32[80,8192]{1,0:T(8,128)} %w_h.1, f32[1,80,8192]{2,1,0:T(8,128)} %g_h.1, f32[80,1,4096]{2,1,0:T(1,128)} %f_h.1, f32[80,1,4096]{2,1,0:T(1,128)} %s_h.1), custom_call_target="tpu_custom_call" | custom-call | tf_op jit(solution)/shard_map/pallas_call | solution.py:272
  142.7 2.4 %shard_map.68 = (f32[80,8192]{1,0:T(8,128)}, f32[80,1,4096]{2,1,0:T(1,128)}, f32[80,1,4096]{2,1,0:T(1,128)}) custom-call(f32[80,8192]{1,0:T(8,128)S(1)} %get-tuple-element.6.nw, f32[80,4096]{1,0:T(8,128)S(1)} %get-tuple-element.7.nf, f32[80,4096]{1,0:T(8,128)S(1)} %get-tuple-element.8.ns), custom_call_target="tpu_custom_call" | custom-call | tf_op jit(solution)/shard_map/pallas_call | solution.py:307

commit v3 on v2

--- a/solution.py
+++ b/solution.py
@@ -14,6 +14,7 @@
 BLK = 256
 ROWS = 8
 HOPS = 4
+SPARE = 128
 
 def each(low, high, body):
     def step(k, carry):
@@ -26,8 +27,8 @@
 def comm(
     depth, entries, w_h, g_h, f_h, s_h, nw, nf, ns,
     w_own, w_oth, g_own, g_oth, fv, sv, grad, raw, norms, ring1, ring2,
-    st, rs, col, ratio, plane, cst, pn, zn, scale,
-    load, b1s, b1r, b2s, b2r, small_s, small_r,
+    st, rs, col, ratio, plane, cst, pn, zn, scale, spare,
+    load, b1s, b1r, b2s, b2r, small_s, small_r, spare_s, spare_r,
 ):
     rows, half = w_own.shape
     chunks, blocks = rows // ROWS, half // BLK
@@ -51,6 +52,7 @@
         return (z // Z_LO, lat, lax.rem(z, Z_LO) * PLANE + q)
 
     onward = along_z(1 + 6 * lat)
+    partner = along_z(HOPS)
 
     def remote(src, dst, s, r, device):
         return pltpu.make_async_remote_copy(
@@ -59,6 +61,11 @@
 
     def fetch(src, dst, i):
         return pltpu.make_async_copy(src, dst, load.at[i])
+
+    barrier = pltpu.get_barrier_semaphore()
+    for k in range(1, 16):
+        pl.semaphore_signal(barrier, inc=1, device_id=in_plane(k), device_id_type=MESH)
+        pl.semaphore_signal(barrier, inc=1, device_id=column(k), device_id_type=MESH)
 
     fetches = [
         fetch(w_h.at[:, pl.ds(own, half)], w_own, 0),
@@ -71,13 +78,6 @@
     for f in fetches:
         f.start()
 
-    barrier = pltpu.get_barrier_semaphore()
-
-    def greet(k):
-        pl.semaphore_signal(barrier, inc=1, device_id=in_plane(k), device_id_type=MESH)
-        pl.semaphore_signal(barrier, inc=1, device_id=column(k), device_id_type=MESH)
-
-    each(1, 16, greet)
 
     def rows_of(i):
         return pl.ds(pl.multiple_of(i * ROWS, ROWS), ROWS)
@@ -85,12 +85,13 @@
     def bulk1(hop, i):
         at = rows_of(i)
         src = ring1.at[hop - 1, at] if hop else g_h.at[0, at, pl.ds(oth, half)]
-        return remote(src, ring1.at[hop, at], b1s.at[hop, i], b1r.at[hop, i], onward)
+        return remote(src, ring1.at[hop, at], b1s.at[hop], b1r.at[hop, i], onward)
 
     def bulk2(hop, i):
         at = rows_of(i)
-        src = ring2.at[hop - 1, at] if hop else raw.at[at]
-        return remote(src, ring2.at[hop, at], b2s.at[hop, i], b2r.at[hop, i], onward)
+        sent = pl.ds(SPARE, half - SPARE)
+        src = ring2.at[hop - 1, at, sent] if hop else raw.at[at, sent]
+        return remote(src, ring2.at[hop, at, sent], b2s.at[hop], b2r.at[hop, i], onward)
 
     def forward(bulk, hop, low, high):
         def one(i):
@@ -124,23 +125,24 @@
     def scatter(src, dst, stage):
         def copy(k):
             to = lax.rem(q + k, PLANE)
-            return remote(src.at[to], dst.at[q], small_s.at[stage, k], small_r.at[stage, k], in_plane(k))
+            return remote(src.at[to], dst.at[q], small_s.at[stage], small_r.at[stage], in_plane(k))
 
         return copy
 
     def gather(ref, stage):
         def copy(k):
-            return remote(ref.at[q], ref.at[q], small_s.at[stage, k], small_r.at[stage, k], in_plane(k))
+            return remote(ref.at[q], ref.at[q], small_s.at[stage], small_r.at[stage], in_plane(k))
 
         return copy
 
-    def run(copy, low, high):
-        each(low, high, lambda k: copy(k).start())
-        each(low, high, lambda k: copy(k).wait_recv())
+    def messages(ref, count, stage):
+        every = ref.at[pl.ds(0, count)]
+        return remote(every, every, small_s.at[stage], small_r.at[stage], onward)
 
     rs[q] = st[q]
     scatter1 = scatter(st, rs, 0)
-    run(scatter1, 1, PLANE)
+    each(1, PLANE, lambda k: scatter1(k).start())
+    messages(rs, 15, 0).wait_recv()
     col[u, 0:3] = jnp.sum(rs[...], axis=0)
     for hop in range(1, HOPS):
         forward(bulk1, hop, 0, chunks)
@@ -159,9 +161,14 @@
     col[u, 3] = jnp.sum(total, axis=0, keepdims=True)
 
     def gather_z(k):
-        return remote(col.at[u], col.at[u], small_s.at[1, k], small_r.at[1, k], column(k))
-
-    run(gather_z, 1, 16)
+        return remote(col.at[u], col.at[u], small_s.at[1], small_r.at[1], column(k))
+
+    for k in range(1, 16):
+        gather_z(k).start()
+    fetches[4].wait()
+    fetches[5].wait()
+    norms[...] = jnp.zeros_like(norms)
+    messages(col, 15, 1).wait_recv()
     total = jnp.zeros((1, BLK), F32)
     for core in range(2):
         parts = [jnp.sum(col[pl.ds(core * 8 + h * Z_LO, Z_LO)], axis=0) for h in range(2)]
@@ -170,28 +177,38 @@
             ratio[core, h] = inner / parts[h][2]
             total += parts[h][3] - inner * ratio[core, h]
     plane[q, 0] = ratio[lat, dp]
-    plane[q, 1] = total
+    plane[q, 1] = ratio[lat, 1 - dp]
+    plane[q, 2] = total
     gather1 = gather(plane, 2)
-    run(gather1, 1, PLANE)
-    total = jnp.sum(jnp.sum(plane[:, 1], axis=0), axis=1, keepdims=True)
+    for k in range(1, PLANE):
+        gather1(k).start()
+
+    def spare_copy(i):
+        src = (grad, fv, sv)[i].at[:, pl.ds(0, SPARE)]
+        return remote(src, spare.at[i], spare_s, spare_r, partner)
+
+    for i in range(3):
+        spare_copy(i).start()
+    messages(plane, 15, 2).wait_recv()
+    total = jnp.sum(jnp.sum(plane[:, 2], axis=0), axis=1, keepdims=True)
     total = jnp.maximum(total, 0.0)
     clip = jnp.minimum(F32(1.0), 0.5 / jnp.sqrt(total / entries + 1e-06))
 
-    fetches[4].wait()
-    fetches[5].wait()
-    norms[...] = jnp.zeros_like(norms)
+    def step_of(g, ratios, w, f, s):
+        clipped = clip * (g - ratios * w)
+        new_f = 0.9 * f + 0.1 * clipped
+        new_s = 0.999 * s + 0.001 * clipped * clipped
+        return new_f, new_s, w - 0.2 * new_f / (jnp.sqrt(new_s) + 1e-08)
 
     def update(i):
         at = rows_of(i)
         for b in range(blocks):
             cols = pl.ds(b * BLK, BLK)
-            w = w_own[at, cols]
-            clipped = clip * (grad[at, cols] - plane[b, 0] * w)
-            first = 0.9 * fv[at, cols] + 0.1 * clipped
-            second = 0.999 * sv[at, cols] + 0.001 * clipped * clipped
+            first, second, r = step_of(
+                grad[at, cols], plane[b, 0], w_own[at, cols], fv[at, cols], sv[at, cols]
+            )
             nf[at, cols] = first
             ns[at, cols] = second
-            r = w - 0.2 * first / (jnp.sqrt(second) + 1e-08)
             raw[at, cols] = r
             norms[:, cols] += r * r
         bulk2(0, i).start()
@@ -202,22 +219,23 @@
 
     pn[q] = cst[q]
     scatter2 = scatter(cst, pn, 3)
-    run(scatter2, 1, PLANE)
+    each(1, PLANE, lambda k: scatter2(k).start())
+    messages(pn, 15, 3).wait_recv()
     zn[z8] = jnp.sum(pn[...], axis=0)
 
     def gather_n(k):
-        return remote(zn.at[z8], zn.at[z8], small_s.at[4, k], small_r.at[4, k], along_z(k))
+        return remote(zn.at[z8], zn.at[z8], small_s.at[4], small_r.at[4], along_z(k))
 
     each(1, 8, lambda k: gather_n(k).start())
     forward(bulk2, 1, 0, chunks)
     forward(bulk2, 2, 0, chunks // 2)
-    each(1, 8, lambda k: gather_n(k).wait_recv())
+    messages(zn, 7, 4).wait_recv()
     for h in range(2):
         scale[q, h] = lax.rsqrt(jnp.sum(zn[h * Z_LO : (h + 1) * Z_LO], axis=0) / depth + 1e-06)
     gather2 = gather(scale, 5)
     each(1, PLANE, lambda k: gather2(k).start())
     forward(bulk2, 2, chunks // 2, chunks)
-    each(1, PLANE, lambda k: gather2(k).wait_recv())
+    messages(scale, 15, 5).wait_recv()
 
     def finish(src, part, base):
         def step(i):
@@ -228,6 +246,16 @@
 
         return step
 
+    remote(spare, spare, spare_s, spare_r, partner).wait_recv()
+
+    def update_spare(i):
+        at = rows_of(i)
+        cols = pl.ds(0, SPARE)
+        ring2[HOPS - 1, at, cols] = step_of(
+            spare[0, at], plane[0, 1][:, :SPARE], w_oth[at, cols], spare[1, at], spare[2, at]
+        )[2]
+
+    each(0, chunks, update_spare)
     each(0, chunks, finish(raw, dp, own))
     forward(bulk2, 3, 0, chunks)
     last = finish(ring2.at[HOPS - 1], 1 - dp, oth)
@@ -236,14 +264,18 @@
         bulk2(HOPS - 1, i).wait_recv()
         last(i)
 
+    def sent(ref, sems, hop):
+        return remote(ref, ref, sems.at[hop], b1r.at[hop, 0], onward)
+
+    for hop in range(HOPS):
+        sent(ring1.at[hop], b1s, hop).wait_send()
+    for hop in range(HOPS - 1):
+        sent(ring2.at[hop, :, pl.ds(SPARE, half - SPARE)], b2s, hop).wait_send()
+    for stage, (ref, count) in enumerate(((rs, 15), (col, 15), (plane, 15), (pn, 15), (zn, 7), (scale, 15))):
+        messages(ref, count, stage).wait_send()
+    remote(spare, spare, spare_s, spare_r, partner).wait_send()
     each(0, chunks, receive)
-
-    for hop in range(HOPS):
-        each(0, chunks, lambda i: bulk1(hop, i).wait_send())
-        each(0, chunks, lambda i: bulk2(hop, i).wait_send())
-    for copy in (scatter1, gather_z, gather1, scatter2, gather2):
-        each(1, PLANE, lambda k: copy(k).wait_send())
-    each(1, 8, lambda k: gather_n(k).wait_send())
+    sent(ring2.at[HOPS - 1, :, pl.ds(SPARE, half - SPARE)], b2s, HOPS - 1).wait_send()
 
 
 def store(nw, nf, ns, nw_h, nf_h, ns_h, sem):
@@ -287,18 +319,21 @@
                 pltpu.VMEM((PLANE, 3, 1, BLK), F32),
                 pltpu.VMEM((16, 4, 1, BLK), F32),
                 pltpu.VMEM((2, 2, 1, BLK), F32),
-                pltpu.VMEM((PLANE, 2, 1, BLK), F32),
+                pltpu.VMEM((PLANE, 3, 1, BLK), F32),
                 pltpu.VMEM((PLANE, 1, BLK), F32),
                 pltpu.VMEM((PLANE, 1, BLK), F32),
                 pltpu.VMEM((8, 1, BLK), F32),
                 pltpu.VMEM((PLANE, 2, 1, BLK), F32),
+                pltpu.VMEM((3, rows, SPARE), F32),
                 dma((6,)),
+                dma((HOPS,)),
                 dma((HOPS, chunks)),
+                dma((HOPS,)),
                 dma((HOPS, chunks)),
-                dma((HOPS, chunks)),
-                dma((HOPS, chunks)),
-                dma((6, 16)),
-                dma((6, 16)),
+                dma((6,)),
+                dma((6,)),
+                dma,
+                dma,
             ],
             compiler_params=pltpu.CompilerParams(
                 collective_id=0, has_side_effects=True, vmem_limit_bytes=32 << 20

time: 145 us -> 141 us (0.972)
  Pallas kernels: 144 us -> 139 us
    pallas_call x1, Pallas kernels: 142 us -> 137 us  [step(): pl.pallas_call(functools.partial(comm, depth, entries), out_shape=(jax.Sh...]
where the time goes in v3:
time: 141 us; the launch traced here: 140 us
  Pallas kernels  139 us (99%)
    pallas_call x1, Pallas kernels, step(): pl.pallas_call(functools.partial(comm, depth, entries), out_shape=(jax.Sh...  137 us

profile of v3, /device:TPU:2, one launch (start us, length us, event | category | flops | bytes accessed | tf_op | source)
XLA Modules:
  0.0 139.7 jit_solution(2084362531345849726)
XLA Ops:
  0.6 136.7 %shard_map.67 = (f32[80,8192]{1,0:T(8,128)S(1)}, f32[80,4096]{1,0:T(8,128)S(1)}, f32[80,4096]{1,0:T(8,128)S(1)}) custom-call(f32[80,8192]{1,0:T(8,128)} %w_h.1, f32[1,80,8192]{2,1,0:T(8,128)} %g_h.1, f32[80,1,4096]{2,1,0:T(1,128)} %f_h.1, f32[80,1,4096]{2,1,0:T(1,128)} %s_h.1), custom_call_target="tpu_custom_call" | custom-call | tf_op jit(solution)/shard_map/pallas_call | solution.py:304
  137.3 2.4 %shard_map.68 = (f32[80,8192]{1,0:T(8,128)}, f32[80,1,4096]{2,1,0:T(1,128)}, f32[80,1,4096]{2,1,0:T(1,128)}) custom-call(f32[80,8192]{1,0:T(8,128)S(1)} %get-tuple-element.6.nw, f32[80,4096]{1,0:T(8,128)S(1)} %get-tuple-element.7.nf, f32[80,4096]{1,0:T(8,128)S(1)} %get-tuple-element.8.ns), custom_call_target="tpu_custom_call" | custom-call | tf_op jit(solution)/shard_map/pallas_call | solution.py:342

commit v4 on v3

--- a/solution.py
+++ b/solution.py
@@ -12,8 +12,10 @@
 PLANE = 16
 Z_LO = 4
 BLK = 256
-ROWS = 8
+ROWS = 16
 HOPS = 4
+PLANE_ORDER = (10, 6, 14, 9, 11, 2, 8, 5, 7, 13, 15, 1, 3, 4, 12)
+COLUMN_ORDER = (4, 12, 3, 5, 11, 13, 2, 6, 10, 14, 1, 7, 9, 15, 8)
 SPARE = 128
 
 def each(low, high, body):
@@ -63,9 +65,9 @@
         return pltpu.make_async_copy(src, dst, load.at[i])
 
     barrier = pltpu.get_barrier_semaphore()
-    for k in range(1, 16):
+    for k, j in zip(PLANE_ORDER, COLUMN_ORDER):
         pl.semaphore_signal(barrier, inc=1, device_id=in_plane(k), device_id_type=MESH)
-        pl.semaphore_signal(barrier, inc=1, device_id=column(k), device_id_type=MESH)
+        pl.semaphore_signal(barrier, inc=1, device_id=column(j), device_id_type=MESH)
 
     fetches = [
         fetch(w_h.at[:, pl.ds(own, half)], w_own, 0),
@@ -163,7 +165,7 @@
     def gather_z(k):
         return remote(col.at[u], col.at[u], small_s.at[1], small_r.at[1], column(k))
 
-    for k in range(1, 16):
+    for k in COLUMN_ORDER:
         gather_z(k).start()
     fetches[4].wait()
     fetches[5].wait()
@@ -180,7 +182,7 @@
     plane[q, 1] = ratio[lat, 1 - dp]
     plane[q, 2] = total
     gather1 = gather(plane, 2)
-    for k in range(1, PLANE):
+    for k in PLANE_ORDER:
         gather1(k).start()
 
     def spare_copy(i):

time: 141 us -> 140 us (level)
  no operation moved by 1% of the time
where the time goes in v4:
time: 140 us; the launch traced here: 139 us
  Pallas kernels  139 us (99%)
    pallas_call x1, Pallas kernels, step(): pl.pallas_call(functools.partial(comm, depth, entries), out_shape=(jax.Sh...  136 us

profile of v4, /device:TPU:2, one launch (start us, length us, event | category | flops | bytes accessed | tf_op | source)
XLA Modules:
  0.0 139.3 jit_solution(11676916966824021625)
XLA Ops:
  0.6 136.2 %shard_map.67 = (f32[80,8192]{1,0:T(8,128)S(1)}, f32[80,4096]{1,0:T(8,128)S(1)}, f32[80,4096]{1,0:T(8,128)S(1)}) custom-call(f32[80,8192]{1,0:T(8,128)} %w_h.1, f32[1,80,8192]{2,1,0:T(8,128)} %g_h.1, f32[80,1,4096]{2,1,0:T(1,128)} %f_h.1, f32[80,1,4096]{2,1,0:T(1,128)} %s_h.1), custom_call_target="tpu_custom_call" | custom-call | tf_op jit(solution)/shard_map/pallas_call | solution.py:306
  136.9 2.4 %shard_map.68 = (f32[80,8192]{1,0:T(8,128)}, f32[80,1,4096]{2,1,0:T(1,128)}, f32[80,1,4096]{2,1,0:T(1,128)}) custom-call(f32[80,8192]{1,0:T(8,128)S(1)} %get-tuple-element.6.nw, f32[80,4096]{1,0:T(8,128)S(1)} %get-tuple-element.7.nf, f32[80,4096]{1,0:T(8,128)S(1)} %get-tuple-element.8.ns), custom_call_target="tpu_custom_call" | custom-call | tf_op jit(solution)/shard_map/pallas_call | solution.py:344
